TPU v7x, 32 devices: a whole 2x2x4 slice. The times are simulated.
32 devices in a mesh: row: 8 (over z, y), col: 4 (over x, core).
Axes of the slice: x: 2, y: 2, z: 4, core: 2. Of those that a mesh axis runs over, the one named last changes fastest.
Arguments:
- start_block: float32 [64, 16, 128], P(('row', 'col')), may hold values from -6 to 6
- blocks: float32 [8, 4, 58, 128, 128], P('row', 'col'), as said below
- slot_row: int32 [8, 4, 58], P('row', 'col'), may hold values from 0 to 7, as said below
- slot_col: int32 [8, 4, 58], P('row', 'col'), may hold values from 0 to 15, as said below
- counts: int32 [8, 4], P('row', 'col'), may hold values from 34 to 58, as said below
Outputs:
- alphas: float32 [2, 16, 16], replicated
- betas: float32 [2, 16, 16], replicated
- next_block: float32 [64, 16, 128], P(('row', 'col'))
Inputs may be any that keep to these rules, and one draw needn't show every extreme that they name: `blocks`: over all cells the live slots list each nonzero block of a symmetric matrix exactly once: block (J, I) is listed exactly when (I, J) is, holding its transpose. Slots at or past a cell's count hold finite values that are no part of H. `counts`: live slots of a cell come first; in every draw some cell has all 58 slots live. `slot_row`: for live slots, the block row within the cell's row group of 8 block rows. `slot_col`: for live slots, the position within the cell's column group of 16 block columns, as in the first step.
All inputs are finite; a program needn't handle non-finite values.
Results may differ from a plain program's by a relative error of at most 0.0003.
Values sent between devices are 32-bit elements; how exact they have to be, the bound alone decides.
A program may use at most 64 MiB of HBM per device.

v0:
```python
import jax
import jax.numpy as jnp
from jax import lax
from jax.sharding import PartitionSpec as P

ITERS = 2
highest = lax.Precision.HIGHEST


def matmul(left, right):
    return jnp.dot(left, right, precision=highest, preferred_element_type=jnp.float32)


def local_gram(left, right):
    return jnp.einsum(
        "bki,bli->kl", left, right, precision=highest, preferred_element_type=jnp.float32
    )


def on_device(start_block, blocks, slot_row, slot_col, counts):
    matrix_tiles = blocks[0, 0]
    rows_local = slot_row[0, 0]
    cols_local = slot_col[0, 0]
    capacity = matrix_tiles.shape[0]
    active = lax.iota(jnp.int32, capacity) < counts[0, 0]
    piece_rows = start_block.shape[0]
    vec_count = start_block.shape[1]
    orbitals = start_block.shape[2]
    row_total = float(piece_rows * lax.axis_size("row") * lax.axis_size("col") * orbitals)
    identity = jnp.eye(vec_count, dtype=jnp.float32)
    start_mean = lax.psum(local_gram(start_block, start_block), ("row", "col")) / row_total
    factor = jnp.linalg.cholesky(start_mean)
    inverse = jax.scipy.linalg.solve_triangular(factor, identity, lower=True)
    vectors = jnp.einsum(
        "kl,bli->bki", inverse, start_block, precision=highest, preferred_element_type=jnp.float32
    )
    previous = jnp.zeros(vectors.shape, jnp.float32)
    beta_prev = jnp.zeros((vec_count, vec_count), jnp.float32)
    alpha_list = []
    beta_list = []
    for iteration in range(ITERS):
        gathered = lax.all_gather(vectors, "row", axis=0, tiled=True)
        operate_product = jnp.einsum(
            "sij,skj->ski",
            matrix_tiles,
            gathered[cols_local],
            precision=highest,
            preferred_element_type=jnp.float32,
        )
        targets = lax.iota(jnp.int32, lax.axis_size("col") * piece_rows)
        selector = ((rows_local[None, :] == targets[:, None]) & active[None, :]).astype(jnp.float32)
        image_block = lax.psum_scatter(
            jnp.einsum(
                "rs,ski->rki",
                selector,
                operate_product,
                precision=highest,
                preferred_element_type=jnp.float32,
            ),
            "col",
            scatter_dimension=0,
            tiled=True,
        )
        stacked = jnp.concatenate([image_block, vectors, previous], axis=1)
        all_means = lax.psum(local_gram(stacked, stacked), ("row", "col")) / row_total
        yy_mean = all_means[:vec_count, :vec_count]
        vy_mean = all_means[vec_count : 2 * vec_count, :vec_count]
        py_mean = all_means[2 * vec_count :, :vec_count]
        vv_mean = all_means[vec_count : 2 * vec_count, vec_count : 2 * vec_count]
        pv_mean = all_means[2 * vec_count :, vec_count : 2 * vec_count]
        pp_mean = all_means[2 * vec_count :, 2 * vec_count :]
        residual = image_block - jnp.einsum(
            "lk,bli->bki", vy_mean, vectors, precision=highest, preferred_element_type=jnp.float32
        )
        residual = residual - jnp.einsum(
            "kl,bli->bki",
            beta_prev,
            previous,
            precision=highest,
            preferred_element_type=jnp.float32,
        )
        gram_mean = yy_mean - matmul(vy_mean.T, vy_mean) - matmul(vy_mean.T, vy_mean)
        gram_mean = gram_mean + matmul(matmul(vy_mean.T, vv_mean), vy_mean)
        gram_mean = gram_mean - matmul(py_mean.T, beta_prev.T) - matmul(beta_prev, py_mean)
        gram_mean = gram_mean + matmul(matmul(vy_mean.T, pv_mean.T), beta_prev.T)
        gram_mean = gram_mean + matmul(matmul(beta_prev, pv_mean), vy_mean)
        gram_mean = gram_mean + matmul(matmul(beta_prev, pp_mean), beta_prev.T)
        factor = jnp.linalg.cholesky(gram_mean)
        beta_block = factor.T
        inverse = jax.scipy.linalg.solve_triangular(factor, identity, lower=True)
        previous = vectors
        vectors = jnp.einsum(
            "kl,bli->bki", inverse, residual, precision=highest, preferred_element_type=jnp.float32
        )
        beta_prev = beta_block
        alpha_list.append(vy_mean)
        beta_list.append(beta_block)
    return (jnp.stack(alpha_list), jnp.stack(beta_list), vectors)


def solution(mesh):
    placed = (
        P(("row", "col"), None, None),
        P("row", "col", None, None, None),
        P("row", "col", None),
        P("row", "col", None),
        P("row", "col"),
    )
    return jax.shard_map(
        on_device,
        mesh=mesh,
        in_specs=placed,
        out_specs=(P(), P(), P(("row", "col"), None, None)),
        check_vma=False,
    )
```

profile of v0, /device:TPU:0, one launch (start us, length us, event | category | flops | bytes accessed | tf_op | source)
XLA Modules:
  0.0 285.7 jit_solution(17474431526224107313)
XLA Ops:
  7.9 0.7 fusion.84
  8.6 0.1 convolution_bitcast_fusion.12
  8.7 42.0 %psum.21 = f32[16,16]{0,1:T(8,128)S(1)} all-reduce(f32[16,16]{0,1:T(8,128)S(1)} %convolution_bitcast_fusion.12), channel_id=1, replica_groups=mesh['row'=8,'col'=4] {'row','col'}, use_global_device_ids=true, to_apply=%region_0.0 | all-reduce | flops 256 | bytes 2048 | tf_op jit(solution)/shard_map/psum | solution.py:31
  50.8 1.5 cholesky.59
  52.3 0.6 compare_reduce_fusion.2
  52.9 0.6 fusion.25
  53.6 1.2 custom-call.7
  54.8 0.2 convolution_bitcast_fusion.11
  55.0 0.1 convolution_bitcast_fusion.8
  55.1 30.6 %all_gather.6 = f32[16,16,128]{2,1,0:T(8,128)S(1)} all-gather(f32[2,16,128]{2,1,0:T(8,128)S(1)} %convolution_bitcast_fusion.8), channel_id=1, replica_groups=mesh['row'=8,'col'=4] {'row'}, dimensions={0}, use_global_device_ids=true | all-gather | bytes 147456 | tf_op jit(solution)/shard_map/all_gather | solution.py:42
  85.7 0.6 gather_fusion
  86.4 8.1 %fusion.2 = f32[58,16,128]{2,1,0:T(8,128)S(1)} fusion(f32[58,16,128]{2,1,0:T(8,128)S(1)} %gather_fusion, f32[1,1,58,128,128]{4,3,2,1,0:T(8,128)} %param.9), kind=kOutput, calls=%fused_computation.4 | convolution fusion | flops 182452224 | bytes 4751360 | tf_op jit(solution)/shard_map/sij,skj->ski/dot_general | solution.py:43
  94.4 0.4 fusion.10
  94.8 0.6 copy.36
  95.6 19.3 %reduce-scatter.3.cloned.1.call-done = f32[2,16,128]{2,1,0:T(8,128)} async-done(((f32[8,16,128]{2,1,0:T(8,128)}), f32[2,16,128]{2,1,0:T(8,128)}) %reduce-scatter.3.cloned.1.call-update) | async-done | bytes 16400 | tf_op jit(solution)/shard_map/reduce_scatter | solution.py:52
  114.9 1.0 convolution_bitcast_fusion.1
  115.9 39.5 %psum.22 = f32[48,48]{0,1:T(8,128)S(1)} all-reduce(f32[48,48]{0,1:T(8,128)S(1)} %convolution_bitcast_fusion.1), channel_id=1, replica_groups=mesh['row'=8,'col'=4] {'row','col'}, use_global_device_ids=true, to_apply=%region_4.0 | all-reduce | flops 2304 | bytes 18432 | tf_op jit(solution)/shard_map/psum | solution.py:65
  155.4 0.2 fusion.50
  155.6 0.2 fusion.30
  155.8 0.2 fusion.52
  156.0 0.2 fusion.32
  156.2 0.2 subtract_subtract_fusion.1
  156.4 0.9 fusion.7
  157.5 0.2 convolution_add_fusion.7
  157.7 0.2 convolution_subtract_fusion.3
  157.9 0.2 convolution_subtract_fusion.2
  158.1 0.1 convolution_add_fusion.6
  158.2 0.2 convolution_add_fusion.5
  158.4 0.1 convolution_add_fusion.4
  158.7 1.5 cholesky.70
  160.2 0.6 compare_reduce_fusion.1
  160.8 0.6 fusion.94
  161.5 1.2 custom-call.8
  162.7 0.2 convolution_bitcast_fusion.10
  162.9 0.1 convolution_bitcast_fusion.5
  163.0 30.7 %all_gather.7 = f32[16,16,128]{2,1,0:T(8,128)S(1)} all-gather(f32[2,16,128]{2,1,0:T(8,128)S(1)} %convolution_bitcast_fusion.5), channel_id=1, replica_groups=mesh['row'=8,'col'=4] {'row'}, dimensions={0}, use_global_device_ids=true | all-gather | bytes 147456 | tf_op jit(solution)/shard_map/all_gather | solution.py:42
  193.8 0.6 gather_fusion.1
  194.4 8.1 %fusion = f32[58,16,128]{2,1,0:T(8,128)S(1)} fusion(f32[58,16,128]{2,1,0:T(8,128)S(1)} %gather_fusion.1, f32[1,1,58,128,128]{4,3,2,1,0:T(8,128)} %param.9), kind=kOutput, calls=%fused_computation.2 | convolution fusion | flops 182452224 | bytes 4751360 | tf_op jit(solution)/shard_map/sij,skj->ski/dot_general | solution.py:43
  202.5 0.4 fusion.8
  202.9 0.6 copy.47
  203.6 20.4 %reduce-scatter.5.cloned.1.call-done = f32[2,16,128]{2,1,0:T(8,128)} async-done(((f32[8,16,128]{2,1,0:T(8,128)}), f32[2,16,128]{2,1,0:T(8,128)}) %reduce-scatter.5.cloned.1.call-update) | async-done | bytes 16400 | tf_op jit(solution)/shard_map/reduce_scatter | solution.py:52
  223.9 1.0 convolution_bitcast_fusion
  224.9 39.5 %psum.23 = f32[48,48]{0,1:T(8,128)S(1)} all-reduce(f32[48,48]{0,1:T(8,128)S(1)} %convolution_bitcast_fusion), channel_id=1, replica_groups=mesh['row'=8,'col'=4] {'row','col'}, use_global_device_ids=true, to_apply=%region_6.9 | all-reduce | flops 2304 | bytes 18432 | tf_op jit(solution)/shard_map/psum | solution.py:65
  264.4 0.8 fusion.44
  265.3 0.9 fusion.26
  266.1 0.2 fusion.46
  266.4 0.2 fusion.28
  266.6 0.2 subtract_subtract_fusion
  266.9 0.9 fusion.5
  267.8 0.8 fusion.4
  268.6 0.2 convolution_add_fusion.3
  268.8 0.9 convolution_subtract_fusion.1
  269.7 0.9 convolution_subtract_fusion
  270.6 0.7 copy.58
  271.2 0.8 convolution_add_fusion.2
  272.1 0.2 convolution_add_fusion.1
  272.3 0.9 convolution_add_fusion
  273.2 1.5 cholesky.81
  274.7 0.6 compare_reduce_fusion
  275.4 0.6 select_bitcast_fusion
  276.0 1.2 custom-call.9
  277.2 0.2 convolution_bitcast_fusion.9
  277.5 0.7 copy.59
  278.2 0.7 convolution_bitcast_fusion.2
  (28 shorter events, 0.8 us)
Async XLA Ops:
  7.2 1.4 copy-start
  7.2 87.3 %copy-start.1 = (s32[1,1,58]{2,1,0:T(1,128)S(1)}, s32[1,1,58]{2,1,0:T(1,128)}, u32[]{:S(2)}) copy-start(s32[1,1,58]{2,1,0:T(1,128)} %param.10) | copy-start | bytes 700
  7.2 107.7 %reduce-scatter.3.cloned.1.call-start = ((), (), s32[]{:S(2)}) async-start(), calls=%async_computation.2 | async-start | bytes 81920 | tf_op jit(solution)/shard_map/reduce_scatter | solution.py:52
  95.5 128.4 %reduce-scatter.5.cloned.1.call-start = ((), (), s32[]{:S(2)}) async-start(), calls=%async_computation.3 | async-start | bytes 81920 | tf_op jit(solution)/shard_map/reduce_scatter | solution.py:52
Sparse Core Ops, SparseCore 0:
  95.6 19.2 reduce-scatter.2
  203.6 20.2 reduce-scatter.4
where the time goes:
time: 287 us; the launch traced here: 286 us
  blocking collectives  182 us (63%)
  waiting for transfers between devices  39.7 us (14%)
  matrix products  31.8 us (11%)
  between operations  14.8 us (5%)
  other arithmetic  12.8 us (4%)
  local copies, waits for them, and re-layouts  4.25 us (1%)
    psum x2, blocking collectives, on_device(): lax.psum(local_gram(stacked, stacked), ('row', 'col')) / row_total  79 us
    all_gather x2, blocking collectives, on_device(): gathered = lax.all_gather(vectors, 'row', axis=0, tiled=True)  61.3 us
    psum x1, blocking collectives, on_device(): lax.psum(local_gram(start_block, start_block), ('row', 'col')) / row_total  42 us
    reduce_scatter x2, waiting for transfers between devices, on_device(): lax.psum_scatter(jnp.einsum('rs,ski->rki', selector, operate_product, pre...  39.7 us
    dot_general x2, matrix products, on_device(): jnp.einsum('sij,skj->ski', matrix_tiles, gathered[cols_local], precision=...  16.1 us
    dot_general x22, matrix products, matmul(): jnp.dot(left, right, precision=highest, preferred_element_type=jnp.float32)  8.28 us
  transfers between devices with their start and end apart: 2, of which 2 were waited for; matrix products, arithmetic and copies ran while one was open for 0% of the time, Pallas kernels for 0%

commit v1 on v0

--- a/solution.py
+++ b/solution.py
@@ -39,7 +39,15 @@
     alpha_list = []
     beta_list = []
     for iteration in range(ITERS):
-        gathered = lax.all_gather(vectors, "row", axis=0, tiled=True)
+        ways, here = (lax.axis_size("row"), lax.axis_index("row"))
+        grown, reach = (vectors, 1)
+        while reach < ways:
+            theirs = lax.ppermute(grown, "row", [(d, d ^ reach) for d in range(ways)])
+            mine_first = jnp.concatenate([grown, theirs], axis=0)
+            theirs_first = jnp.concatenate([theirs, grown], axis=0)
+            grown = jnp.where(here & reach == 0, mine_first, theirs_first)
+            reach = 2 * reach
+        gathered = grown
         operate_product = jnp.einsum(
             "sij,skj->ski",
             matrix_tiles,

time: 287 us -> 254 us (0.89)
  blocking collectives: 182 us -> 121 us
  waiting for transfers between devices: 39.7 us -> 54.2 us
  starting transfers between devices: 0.08 us -> 12.8 us
    all_gather x2 -> x0, blocking collectives: 61.3 us -> none  [on_device(): gathered = lax.all_gather(vectors, 'row', axis=0, tiled=True)]
    ppermute x0 -> x6, starting transfers between devices: none -> 12.7 us  [on_device(): theirs = lax.ppermute(grown, 'row', [(d, d ^ reach) for d in range(ways)])]
    ppermute x0 -> x6, waiting for transfers between devices: none -> 12.3 us  [on_device(): theirs = lax.ppermute(grown, 'row', [(d, d ^ reach) for d in range(ways)])]
  transfers between devices with their start and end apart: 2 -> 8, of which waited for: 2 -> 8; matrix products, arithmetic and copies ran while one was open for 0% -> 0% of each run, Pallas kernels for 0% -> 0%
where the time goes in v1:
time: 254 us; the launch traced here: 253 us
  blocking collectives  121 us (48%)
  waiting for transfers between devices  54.2 us (21%)
  matrix products  31.8 us (13%)
  between operations  14.8 us (6%)
  starting transfers between devices  12.8 us (5%)
  other arithmetic  12.8 us (5%)
  local copies, waits for them, and re-layouts  4.91 us (2%)
    psum x2, blocking collectives, on_device(): lax.psum(local_gram(stacked, stacked), ('row', 'col')) / row_total  79.2 us
    psum x1, blocking collectives, on_device(): lax.psum(local_gram(start_block, start_block), ('row', 'col')) / row_total  42 us
    reduce_scatter x2, waiting for transfers between devices, on_device(): lax.psum_scatter(jnp.einsum('rs,ski->rki', selector, operate_product, pre...  41.9 us
    dot_general x2, matrix products, on_device(): jnp.einsum('sij,skj->ski', matrix_tiles, gathered[cols_local], precision=...  16.1 us
    ppermute x6, starting transfers between devices, on_device(): theirs = lax.ppermute(grown, 'row', [(d, d ^ reach) for d in range(ways)])  12.7 us
    ppermute x6, waiting for transfers between devices, on_device(): theirs = lax.ppermute(grown, 'row', [(d, d ^ reach) for d in range(ways)])  12.3 us
    dot_general x22, matrix products, matmul(): jnp.dot(left, right, precision=highest, preferred_element_type=jnp.float32)  8.28 us
  transfers between devices with their start and end apart: 8, of which 8 were waited for; matrix products, arithmetic and copies ran while one was open for 0% of the time, Pallas kernels for 0%

profile of v1, /device:TPU:0, one launch (start us, length us, event | category | flops | bytes accessed | tf_op | source)
XLA Modules:
  0.0 252.6 jit_solution(13639942345890395916)
XLA Ops:
  7.2 0.7 copy-done
  8.0 42.0 %psum.21 = f32[16,16]{0,1:T(8,128)S(1)} all-reduce(f32[16,16]{0,1:T(8,128)S(1)} %convolution_bitcast_fusion.12), channel_id=1, replica_groups=mesh['row'=8,'col'=4] {'row','col'}, use_global_device_ids=true, to_apply=%region_0.0 | all-reduce | flops 256 | bytes 2048 | tf_op jit(solution)/shard_map/psum | solution.py:31
  50.1 1.5 cholesky.59
  51.6 0.6 compare_reduce_fusion.2
  52.2 0.6 fusion.25
  52.9 1.2 custom-call.7
  54.1 0.2 convolution_bitcast_fusion.11
  54.5 2.3 collective-permute-start
  56.8 0.7 fusion.84
  57.4 1.1 collective-permute-done
  58.5 1.5 collective-permute-start.1
  60.7 1.8 collective-permute-done.1
  62.4 2.6 %collective-permute-start.2 = (f32[8,16,128]{2,1,0:T(8,128)S(1)}, f32[8,16,128]{2,1,0:T(8,128)S(1)}, u32[]{:S(2)}, u32[]{:S(2)}) collective-permute-start(f32[8,16,128]{2,1,0:T(8,128)S(1)} %maximum_select_fusion.2), channel_id=1, source_target_pairs={{0,16},{4,20},{8,24},{12,28},{16,0},{20,4},{24,8},{28,12},{1,17},{... | collective-permute-start | bytes 196616 | tf_op jit(solution)/shard_map/ppermute | solution.py:45
  65.1 2.6 %collective-permute-done.2 = f32[8,16,128]{2,1,0:T(8,128)S(1)} collective-permute-done((f32[8,16,128]{2,1,0:T(8,128)S(1)}, f32[8,16,128]{2,1,0:T(8,128)S(1)}, u32[]{:S(2)}, u32[]{:S(2)}) %collective-permute-start.2) | collective-permute-done | bytes 65568 | tf_op jit(solution)/shard_map/ppermute | solution.py:45
  67.7 0.6 gather_fusion
  68.3 8.1 %fusion.2 = f32[58,16,128]{2,1,0:T(8,128)S(1)} fusion(f32[58,16,128]{2,1,0:T(8,128)S(1)} %gather_fusion, f32[1,1,58,128,128]{4,3,2,1,0:T(8,128)} %param.9), kind=kOutput, calls=%fused_computation.4 | convolution fusion | flops 182452224 | bytes 4751360 | tf_op jit(solution)/shard_map/sij,skj->ski/dot_general | solution.py:51
  76.4 0.4 fusion.10
  76.8 0.6 copy.10
  77.5 20.5 %reduce-scatter.3.cloned.1.call-done = f32[2,16,128]{2,1,0:T(8,128)} async-done(((f32[8,16,128]{2,1,0:T(8,128)}), f32[2,16,128]{2,1,0:T(8,128)}) %reduce-scatter.3.cloned.1.call-update) | async-done | bytes 16400 | tf_op jit(solution)/shard_map/reduce_scatter | solution.py:60
  98.0 1.0 convolution_bitcast_fusion.1
  98.9 39.7 %psum.22 = f32[48,48]{0,1:T(8,128)S(1)} all-reduce(f32[48,48]{0,1:T(8,128)S(1)} %convolution_bitcast_fusion.1), channel_id=1, replica_groups=mesh['row'=8,'col'=4] {'row','col'}, use_global_device_ids=true, to_apply=%region_4.7 | all-reduce | flops 2304 | bytes 18432 | tf_op jit(solution)/shard_map/psum | solution.py:73
  139.0 0.2 fusion.52
  139.2 0.2 fusion.32
  139.4 0.2 subtract_subtract_fusion.1
  139.7 0.9 fusion.7
  140.9 0.2 convolution_subtract_fusion.3
  141.5 0.2 convolution_add_fusion.5
  141.9 1.5 cholesky.70
  143.4 0.6 compare_reduce_fusion.1
  144.1 0.6 fusion.94
  144.7 1.2 custom-call.8
  145.9 0.2 convolution_bitcast_fusion.10
  146.3 2.3 collective-permute-start.3
  148.6 1.7 collective-permute-done.3
  150.4 1.5 collective-permute-start.4
  151.8 2.5 collective-permute-done.4
  154.3 2.5 collective-permute-start.5
  156.8 2.8 %collective-permute-done.5 = f32[8,16,128]{2,1,0:T(8,128)S(1)} collective-permute-done((f32[8,16,128]{2,1,0:T(8,128)S(1)}, f32[8,16,128]{2,1,0:T(8,128)S(1)}, u32[]{:S(2)}, u32[]{:S(2)}) %collective-permute-start.5) | collective-permute-done | bytes 65568 | tf_op jit(solution)/shard_map/ppermute | solution.py:45
  159.5 0.6 gather_fusion.1
  160.2 8.1 %fusion = f32[58,16,128]{2,1,0:T(8,128)S(1)} fusion(f32[58,16,128]{2,1,0:T(8,128)S(1)} %gather_fusion.1, f32[1,1,58,128,128]{4,3,2,1,0:T(8,128)} %param.9), kind=kOutput, calls=%fused_computation.2 | convolution fusion | flops 182452224 | bytes 4751360 | tf_op jit(solution)/shard_map/sij,skj->ski/dot_general | solution.py:51
  168.2 0.4 fusion.8
  168.6 0.6 copy.21
  169.4 21.4 %reduce-scatter.5.cloned.1.call-done = f32[2,16,128]{2,1,0:T(8,128)} async-done(((f32[8,16,128]{2,1,0:T(8,128)}), f32[2,16,128]{2,1,0:T(8,128)}) %reduce-scatter.5.cloned.1.call-update) | async-done | bytes 16400 | tf_op jit(solution)/shard_map/reduce_scatter | solution.py:60
  190.8 1.0 convolution_bitcast_fusion
  191.8 39.5 %psum.23 = f32[48,48]{0,1:T(8,128)S(1)} all-reduce(f32[48,48]{0,1:T(8,128)S(1)} %convolution_bitcast_fusion), channel_id=1, replica_groups=mesh['row'=8,'col'=4] {'row','col'}, use_global_device_ids=true, to_apply=%region_6.9 | all-reduce | flops 2304 | bytes 18432 | tf_op jit(solution)/shard_map/psum | solution.py:73
  231.3 0.8 fusion.44
  232.1 0.9 fusion.26
  233.0 0.2 fusion.46
  233.2 0.2 fusion.28
  233.4 0.2 subtract_subtract_fusion
  233.7 0.9 fusion.5
  234.6 0.8 fusion.4
  235.7 0.9 convolution_subtract_fusion.1
  236.5 0.9 convolution_subtract_fusion
  237.4 0.7 copy.32
  238.1 0.8 convolution_add_fusion.2
  239.1 0.9 convolution_add_fusion
  240.1 1.5 cholesky.81
  241.6 0.6 compare_reduce_fusion
  242.2 0.6 select_bitcast_fusion
  242.9 1.2 custom-call.9
  244.1 0.2 convolution_bitcast_fusion.9
  244.3 0.7 copy.33
  245.0 0.7 convolution_bitcast_fusion.2
  (44 shorter events, 2.7 us)
Async XLA Ops:
  7.2 0.7 copy-start
  7.2 69.2 %copy-start.1 = (s32[1,1,58]{2,1,0:T(1,128)S(1)}, s32[1,1,58]{2,1,0:T(1,128)}, u32[]{:S(2)}) copy-start(s32[1,1,58]{2,1,0:T(1,128)} %param.10) | copy-start | bytes 700
  7.2 90.8 %reduce-scatter.3.cloned.1.call-start = ((), (), s32[]{:S(2)}) async-start(), calls=%async_computation.2 | async-start | bytes 81920 | tf_op jit(solution)/shard_map/reduce_scatter | solution.py:60
  54.5 4.0 %collective-permute-start = (f32[2,16,128]{2,1,0:T(8,128)S(1)}, f32[2,16,128]{2,1,0:T(8,128)S(1)}, u32[]{:S(2)}, u32[]{:S(2)}) collective-permute-start(f32[2,16,128]{2,1,0:T(8,128)S(1)} %convolution_bitcast_fusion.8), channel_id=1, source_target_pairs={{0,4},{4,0},{8,12},{12,8},{16,20},{20,16},{24,28},{28,24},{1,5},{5... | collective-permute-start | bytes 49160 | tf_op jit(solution)/shard_map/ppermute | solution.py:45
  58.5 3.9 %collective-permute-start.1 = (f32[4,16,128]{2,1,0:T(8,128)S(1)}, f32[4,16,128]{2,1,0:T(8,128)S(1)}, u32[]{:S(2)}, u32[]{:S(2)}) collective-permute-start(f32[4,16,128]{2,1,0:T(8,128)S(1)} %maximum_select_fusion.4), channel_id=1, source_target_pairs={{0,8},{4,12},{8,0},{12,4},{16,24},{20,28},{24,16},{28,20},{1,9},{5... | collective-permute-start | bytes 98312 | tf_op jit(solution)/shard_map/ppermute | solution.py:45
  62.4 5.2 %collective-permute-start.2 = (f32[8,16,128]{2,1,0:T(8,128)S(1)}, f32[8,16,128]{2,1,0:T(8,128)S(1)}, u32[]{:S(2)}, u32[]{:S(2)}) collective-permute-start(f32[8,16,128]{2,1,0:T(8,128)S(1)} %maximum_select_fusion.2), channel_id=1, source_target_pairs={{0,16},{4,20},{8,24},{12,28},{16,0},{20,4},{24,8},{28,12},{1,17},{... | collective-permute-start | bytes 196616 | tf_op jit(solution)/shard_map/ppermute | solution.py:45
  77.4 113.3 %reduce-scatter.5.cloned.1.call-start = ((), (), s32[]{:S(2)}) async-start(), calls=%async_computation.3 | async-start | bytes 81920 | tf_op jit(solution)/shard_map/reduce_scatter | solution.py:60
  146.3 4.1 %collective-permute-start.3 = (f32[2,16,128]{2,1,0:T(8,128)S(1)}, f32[2,16,128]{2,1,0:T(8,128)S(1)}, u32[]{:S(2)}, u32[]{:S(2)}) collective-permute-start(f32[2,16,128]{2,1,0:T(8,128)S(1)} %convolution_bitcast_fusion.5), channel_id=1, source_target_pairs={{0,4},{4,0},{8,12},{12,8},{16,20},{20,16},{24,28},{28,24},{1,5},{5... | collective-permute-start | bytes 49160 | tf_op jit(solution)/shard_map/ppermute | solution.py:45
  150.4 3.9 %collective-permute-start.4 = (f32[4,16,128]{2,1,0:T(8,128)S(1)}, f32[4,16,128]{2,1,0:T(8,128)S(1)}, u32[]{:S(2)}, u32[]{:S(2)}) collective-permute-start(f32[4,16,128]{2,1,0:T(8,128)S(1)} %maximum_select_fusion.5), channel_id=1, source_target_pairs={{0,8},{4,12},{8,0},{12,4},{16,24},{20,28},{24,16},{28,20},{1,9},{5... | collective-permute-start | bytes 98312 | tf_op jit(solution)/shard_map/ppermute | solution.py:45
  154.3 5.2 %collective-permute-start.5 = (f32[8,16,128]{2,1,0:T(8,128)S(1)}, f32[8,16,128]{2,1,0:T(8,128)S(1)}, u32[]{:S(2)}, u32[]{:S(2)}) collective-permute-start(f32[8,16,128]{2,1,0:T(8,128)S(1)} %maximum_select_fusion.3), channel_id=1, source_target_pairs={{0,16},{4,20},{8,24},{12,28},{16,0},{20,4},{24,8},{28,12},{1,17},{... | collective-permute-start | bytes 196616 | tf_op jit(solution)/shard_map/ppermute | solution.py:45
Sparse Core Ops, SparseCore 0:
  77.6 20.3 reduce-scatter.2
  169.4 21.3 reduce-scatter.4
